TPU v7x, 32 devices: a whole 2x2x4 slice. The times are simulated.
32 devices in a mesh: frame: 8 (over z, core), tok: 4 (over y, x).
Axes of the slice: x: 2, y: 2, z: 4, core: 2. Of those that a mesh axis runs over, the one named last changes fastest.
Arguments:
- stream: bfloat16 [8, 1024, 1152], P('frame', 'tok'), may hold values from -20 to 20
- queries: bfloat16 [8, 1024, 1152], P('frame', 'tok'), may hold values from -200 to 200
- key_vectors: bfloat16 [8, 1024, 1152], P('frame', 'tok'), may hold values from -6 to 6
- value_vectors: bfloat16 [8, 1024, 1152], P('frame', 'tok'), may hold values from -6 to 6
- modulation: float32 [8, 4, 1152], P('frame'), may hold values from -4 to 4
- output_weight: bfloat16 [1152, 1152], replicated, may hold values from -0.1875 to 0.1875
- output_bias: float32 [1152], replicated, may hold values from -3 to 3
- router_weight: bfloat16 [1152, 8], replicated, may hold values from -0.1875 to 0.1875
- expand_weight: bfloat16 [8, 1152, 4608], P('frame', None, 'tok'), may hold values from -0.1875 to 0.1875
- expand_bias: float32 [8, 4608], P('frame', 'tok'), may hold values from -3 to 3
- reduce_weight: bfloat16 [8, 4608, 1152], P('frame', 'tok'), may hold values from -0.09375 to 0.09375
- reduce_bias: float32 [8, 1152], P('frame'), may hold values from -3 to 3
- counts: int32 [8, 8], P(None, 'frame'), may hold values from 1 to 96, 256 in all within a row
- picked_rows: int32 [8, 8, 96], P(None, 'frame'), may hold values from 0 to 1023, as said below
Outputs:
- layer_out: bfloat16 [8, 1024, 1152], P('frame', 'tok')
Inputs may be any that keep to these rules, and one draw needn't show every extreme that they name: counts[e, g] slots of block (e, g) are used; the counts of one expert sum to 256. The entries of one block picked_rows[e, g, :] are distinct positions among the 1024 tokens of frame g; slots at or beyond counts[e, g] are unused.
All inputs are finite; a program needn't handle non-finite values.
Results may differ from a plain program's by a relative error of at most 0.0055.
Values may be sent and summed in bfloat16 or wider, within the bound.
A program may use at most 64 MiB of HBM per device.

v0:
```python
import math
import jax
import jax.numpy as jnp
from jax import lax
from jax.sharding import PartitionSpec as P

H = 16
HD = 72


def layer_norm(values):
    mean_val = jnp.mean(values, axis=-1, keepdims=True)
    centred = values - mean_val
    variance = jnp.mean(centred * centred, axis=-1, keepdims=True)
    return centred * lax.rsqrt(variance + 1e-06)


def head_attention(operands):
    head_queries, head_keys, head_values = operands
    length = head_queries.shape[1]
    block_rows = min(512, length)
    score_scale = 1.0 / math.sqrt(HD)

    def one_block(first_row):
        query_block = lax.dynamic_slice_in_dim(head_queries, first_row, block_rows, 1)
        scores = (
            lax.dot_general(
                query_block, head_keys, (((0,), (0,)), ((), ())), preferred_element_type=jnp.float32
            )
            * score_scale
        )
        scores = scores - jnp.max(scores, axis=1, keepdims=True)
        exponent = jnp.exp(scores)
        weights = (exponent / jnp.sum(exponent, axis=1, keepdims=True)).astype(jnp.bfloat16)
        return lax.dot_general(
            head_values, weights, (((1,), (1,)), ((), ())), preferred_element_type=jnp.float32
        ).astype(jnp.bfloat16)

    starts = jnp.arange(length // block_rows, dtype=jnp.int32) * block_rows
    blocks = lax.map(one_block, starts)
    return blocks.transpose(1, 0, 2).reshape(head_queries.shape[0], length)


def attend_items(pieces):
    outputs = lax.map(head_attention, (pieces[0][0], pieces[1][0], pieces[2][0]))
    return outputs[None]


def per_device(
    stream,
    queries,
    key_vectors,
    value_vectors,
    modulation,
    output_weight,
    output_bias,
    router_weight,
    expand_weight,
    expand_bias,
    reduce_weight,
    reduce_bias,
    counts,
    picked_rows,
):
    tok_groups = lax.axis_size("tok")
    tok_local = stream.shape[1]
    model_width = stream.shape[2]
    heads_local = H // tok_groups

    def to_heads(tensor):
        return tensor[0].reshape(tok_local, tok_groups, heads_local, HD).transpose(1, 2, 3, 0)

    attended = attend_items(
        (
            lax.all_to_all(to_heads(queries), "tok", split_axis=0, concat_axis=3, tiled=True),
            lax.all_to_all(to_heads(key_vectors), "tok", split_axis=0, concat_axis=3, tiled=True),
            lax.all_to_all(to_heads(value_vectors), "tok", split_axis=0, concat_axis=3, tiled=True),
        )
    )
    returned = lax.all_to_all(attended, "tok", split_axis=3, concat_axis=0, tiled=True)
    attended_rows = returned.transpose(3, 0, 1, 2).reshape(tok_local, model_width)
    projected = (
        jnp.dot(attended_rows, output_weight, preferred_element_type=jnp.float32) + output_bias
    )
    shares = modulation[0]
    residual = (stream[0].astype(jnp.float32) + shares[0] * projected).astype(jnp.bfloat16)
    normed = (layer_norm(residual.astype(jnp.float32)) * (1.0 + shares[2]) + shares[1]).astype(
        jnp.bfloat16
    )
    gate_values = jax.nn.sigmoid(jnp.dot(normed, router_weight, preferred_element_type=jnp.float32))
    slot_count = picked_rows.shape[2]
    local_pos = picked_rows[:, 0, :] - lax.axis_index("tok") * tok_local
    in_use = jnp.arange(slot_count, dtype=jnp.int32)[None, :] < counts
    on_shard = in_use & (local_pos >= 0) & (local_pos < tok_local)
    safe_pos = jnp.clip(local_pos, 0, tok_local - 1)
    chosen = jnp.take(normed, safe_pos, axis=0)
    chosen = jnp.where(on_shard[:, :, None], chosen, jnp.zeros_like(chosen))
    moved = lax.all_to_all(chosen, "frame", split_axis=0, concat_axis=1, tiled=True)
    expert_rows = lax.psum(moved.astype(jnp.float32).astype(jnp.bfloat16), "tok")
    hidden = jax.nn.gelu(
        jnp.einsum("erd,edf->erf", expert_rows, expand_weight, preferred_element_type=jnp.float32)
        + expand_bias[:, None, :],
        approximate=True,
    ).astype(jnp.bfloat16)
    partial_out = jnp.einsum(
        "erf,efd->erd", hidden, reduce_weight, preferred_element_type=jnp.float32
    )
    column_count = model_width // tok_groups
    summed = lax.psum_scatter(
        partial_out.astype(jnp.bfloat16), "tok", scatter_dimension=2, tiled=True
    ).astype(jnp.float32)
    bias_part = lax.dynamic_slice_in_dim(
        reduce_bias, lax.axis_index("tok") * column_count, column_count, 1
    )
    expert_out = (summed + bias_part[:, None, :]).astype(jnp.bfloat16)
    returned_cols = lax.all_to_all(expert_out, "frame", split_axis=1, concat_axis=0, tiled=True)
    returned_rows = lax.all_gather(returned_cols, "tok", axis=2, tiled=True)
    mix_weight = jnp.take_along_axis(gate_values.T, safe_pos, axis=1)
    mix_weight = jnp.where(on_shard, mix_weight, jnp.zeros_like(mix_weight)).astype(jnp.bfloat16)
    targets = jnp.arange(tok_local, dtype=jnp.int32)
    matches = (safe_pos.reshape(-1)[None, :] == targets[:, None]) & on_shard.reshape(-1)[None, :]
    scatter_table = jnp.where(matches, mix_weight.reshape(-1)[None, :], jnp.zeros((), jnp.bfloat16))
    expert_mix = jnp.dot(
        scatter_table, returned_rows.reshape(-1, model_width), preferred_element_type=jnp.float32
    )
    layer_out = (residual.astype(jnp.float32) + shares[3] * expert_mix).astype(jnp.bfloat16)
    return layer_out[None]


def solution(mesh):
    return jax.shard_map(
        per_device,
        mesh=mesh,
        in_specs=(
            P("frame", "tok", None),
            P("frame", "tok", None),
            P("frame", "tok", None),
            P("frame", "tok", None),
            P("frame", None, None),
            P(),
            P(),
            P(),
            P("frame", None, "tok"),
            P("frame", "tok"),
            P("frame", "tok", None),
            P("frame", None),
            P(None, "frame"),
            P(None, "frame", None),
        ),
        out_specs=P("frame", "tok", None),
        check_vma=False,
    )
```

profile of v0, /device:TPU:0, one launch (start us, length us, event | category | flops | bytes accessed | tf_op | source)
XLA Modules:
  0.0 382.8 jit_solution(11425842389973880382)
XLA Ops:
  8.8 5.2 %all-to-all-start = ((bf16[4,4,72,256]{3,2,1,0:T(8,128)(2,1)}), bf16[4,4,72,256]{3,2,1,0:T(8,128)(2,1)S(1)}, u32[]{:S(2)}, u32[]{:S(2)}) async-start(bf16[4,4,72,256]{3,2,1,0:T(8,128)(2,1)} %bitcast.128), calls=%async_computation | async-start | bytes 1179648 | tf_op jit(solution)/shard_map/all_to_all | solution.py:75
  16.1 6.6 %all-to-all-done = bf16[4,4,72,256]{3,2,1,0:T(8,128)(2,1)S(1)} async-done(((bf16[4,4,72,256]{3,2,1,0:T(8,128)(2,1)}), bf16[4,4,72,256]{3,2,1,0:T(8,128)(2,1)S(1)}, u32[]{:S(2)}, u32[]{:S(2)}) %all-to-all-start) | async-done | bytes 589856 | tf_op jit(solution)/shard_map/all_to_all | solution.py:75
  22.7 4.3 %all-to-all-start.1 = ((bf16[4,4,72,256]{3,2,1,0:T(8,128)(2,1)}), bf16[4,4,72,256]{3,2,1,0:T(8,128)(2,1)}, u32[]{:S(2)}, u32[]{:S(2)}) async-start(bf16[4,4,72,256]{3,2,1,0:T(8,128)(2,1)} %bitcast.127), calls=%async_computation.1 | async-start | bytes 1179648 | tf_op jit(solution)/shard_map/all_to_all | solution.py:76
  29.2 5.9 %all-to-all-done.1 = bf16[4,4,72,256]{3,2,1,0:T(8,128)(2,1)} async-done(((bf16[4,4,72,256]{3,2,1,0:T(8,128)(2,1)}), bf16[4,4,72,256]{3,2,1,0:T(8,128)(2,1)}, u32[]{:S(2)}, u32[]{:S(2)}) %all-to-all-start.1) | async-done | bytes 589856 | tf_op jit(solution)/shard_map/all_to_all | solution.py:76
  35.1 4.2 %all-to-all-start.2 = ((bf16[4,4,72,256]{3,2,1,0:T(8,128)(2,1)}), bf16[4,4,72,256]{3,2,1,0:T(8,128)(2,1)}, u32[]{:S(2)}, u32[]{:S(2)}) async-start(bf16[4,4,72,256]{3,2,1,0:T(8,128)(2,1)} %bitcast.126), calls=%async_computation.2 | async-start | bytes 1179648 | tf_op jit(solution)/shard_map/all_to_all | solution.py:77
  40.8 2.4 squeeze.27
  49.6 45.9 %while.21 = (s32[]{:T(128)}, bf16[4,72,1024]{2,1,0:T(8,128)(2,1)}, bf16[4,72,1024]{2,1,0:T(8,128)(2,1)}, bf16[4,72,1024]{2,1,0:T(8,128)(2,1)}, bf16[4,72,1024]{2...) while((s32[]{:T(128)}, bf16[4,72,1024]{2,1,0:T(8,128)(2,1)}, ...), condition=%wide.region_5.6_spmd, body=%wide.region_0.5_spmd.sunk | while | flops 155749376 | bytes 8513900 | solution.py:45
  51.6 8.6 %while.22 = (s32[]{:T(128)}, bf16[2,72,512]{2,1,0:T(8,128)(2,1)S(1)}, s32[2]{0:T(128)S(1)}, bf16[72,1024]{1,0:T(8,128)(2,1)S(1)}, bf16[72,1024]{1,0:T(8,128)(2,1...) while((s32[]{:T(128)}, bf16[2,72,512]{2,1,0:T(8,128)(2,1)S(1)}, ...), condition=%wide.region_4.4_spmd, body=%wide.region_1.3_spmd.sunk | while | flops 155749376 | bytes 6744219 | solution.py:40
  63.1 8.6 %while.22 = (s32[]{:T(128)}, bf16[2,72,512]{2,1,0:T(8,128)(2,1)S(1)}, s32[2]{0:T(128)S(1)}, bf16[72,1024]{1,0:T(8,128)(2,1)S(1)}, bf16[72,1024]{1,0:T(8,128)(2,1...) while((s32[]{:T(128)}, bf16[2,72,512]{2,1,0:T(8,128)(2,1)S(1)}, ...), condition=%wide.region_4.4_spmd, body=%wide.region_1.3_spmd.sunk | while | flops 155749376 | bytes 6744219 | solution.py:40
  74.6 8.6 %while.22 = (s32[]{:T(128)}, bf16[2,72,512]{2,1,0:T(8,128)(2,1)S(1)}, s32[2]{0:T(128)S(1)}, bf16[72,1024]{1,0:T(8,128)(2,1)S(1)}, bf16[72,1024]{1,0:T(8,128)(2,1...) while((s32[]{:T(128)}, bf16[2,72,512]{2,1,0:T(8,128)(2,1)S(1)}, ...), condition=%wide.region_4.4_spmd, body=%wide.region_1.3_spmd.sunk | while | flops 155749376 | bytes 6744219 | solution.py:40
  86.0 8.6 %while.22 = (s32[]{:T(128)}, bf16[2,72,512]{2,1,0:T(8,128)(2,1)S(1)}, s32[2]{0:T(128)S(1)}, bf16[72,1024]{1,0:T(8,128)(2,1)S(1)}, bf16[72,1024]{1,0:T(8,128)(2,1...) while((s32[]{:T(128)}, bf16[2,72,512]{2,1,0:T(8,128)(2,1)S(1)}, ...), condition=%wide.region_4.4_spmd, body=%wide.region_1.3_spmd.sunk | while | flops 155749376 | bytes 6744219 | solution.py:40
  97.9 4.4 %all-to-all-start.3 = ((bf16[1,4,72,1024]{2,1,0,3:T(4,128)(2,1)}), bf16[1,4,72,1024]{2,1,0,3:T(4,128)(2,1)}, u32[]{:S(2)}, u32[]{:S(2)}) async-start(bf16[1,4,72,1024]{2,1,0,3:T(4,128)(2,1)} %bitcast.123), calls=%async_computation.3 | async-start | bytes 2097152 | tf_op jit(solution)/shard_map/all_to_all | solution.py:80
  102.5 11.4 %all-to-all-done.3 = bf16[1,4,72,1024]{2,1,0,3:T(4,128)(2,1)} async-done(((bf16[1,4,72,1024]{2,1,0,3:T(4,128)(2,1)}), bf16[1,4,72,1024]{2,1,0,3:T(4,128)(2,1)}, u32[]{:S(2)}, u32[]{:S(2)}) %all-to-all-start.3) | async-done | bytes 589856 | tf_op jit(solution)/shard_map/all_to_all | solution.py:80
  115.4 3.0 fusion.44
  119.7 3.7 gather_fusion
  125.3 46.8 %all_to_all.87 = bf16[8,96,1152]{2,1,0:T(8,128)(2,1)} all-to-all(bf16[8,96,1152]{2,1,0:T(8,128)(2,1)S(1)} %select_select_fusion), channel_id=1, replica_groups=mesh['frame'=8,'tok'=4] {'frame'}, dimensions={0} | all-to-all | bytes 3538944 | tf_op jit(solution)/shard_map/all_to_all | solution.py:98
  172.8 61.5 %all-reduce.2.cloned.1.call-done = bf16[768,1152]{1,0:T(8,128)(2,1)} async-done(((bf16[768,1152]{1,0:T(8,128)(2,1)}), bf16[768,1152]{1,0:T(8,128)(2,1)}) %all-reduce.2.cloned.1.call-update) | async-done | bytes 1769488 | tf_op jit(solution)/shard_map/psum | solution.py:99
  234.2 8.8 %fusion.15 = bf16[1,768,1152]{2,1,0:T(8,128)(2,1)} fusion(bf16[1,1152,1152]{2,1,0:T(8,128)(2,1)S(1)} %copy-done, bf16[768,1152]{1,0:T(8,128)(2,1)} %all-reduce.2.cloned.1.call-done, bf16[1,1152,1152]{2,1,0:T(8,128)(2,1)} %param.26, f32[1152]{0:T(1024)S(1)} %reduce.5), kind=kOutput, calls=%fused_computation.29 | convolution fusion | flops 4086595584 | bytes 8851968 | tf_op jit(solution)/shard_map/erf,efd->erd/dot_general | solution.py:105
  243.0 8.8 %copy.95 = bf16[1,768,1152]{1,0,2:T(2,128)(2,1)} copy(bf16[1,768,1152]{2,1,0:T(8,128)(2,1)} %fusion.15) | data formatting | bytes 3538944
  251.9 3.5 copy.103
  256.2 31.8 %reduce-scatter.4.cloned.1.call-done = bf16[288,768]{1,0:T(8,128)(2,1)} async-done(((bf16[1152,768]{1,0:T(8,128)(2,1)}), bf16[288,768]{1,0:T(8,128)(2,1)}) %reduce-scatter.4.cloned.1.call-update) | async-done | bytes 442384
  290.4 4.6 %copy.90 = bf16[1,768,288]{2,0,1:T(2,128)(2,1)} copy(bf16[1,768,288]{1,2,0:T(8,128)(2,1)} %add_convert_fusion.1) | data formatting | bytes 884736 | tf_op jit(solution)/shard_map/convert_element_type | solution.py:115
  295.5 6.1 %reduce.13 = bf16[768,288]{1,0:T(8,128)(2,1)} reduce(bf16[768,1,288]{2,1,0:T(2,128)(2,1)} %bitcast.121, bf16[]{:T(256)} %broadcast.265), dimensions={1}, to_apply=%bitcast.92.reduce_sub_computation | reduce | bytes 884738
  301.6 2.6 reshape.249
  304.3 18.3 %all_to_all.88 = bf16[8,2,13824]{2,1,0:T(2,128)(2,1)} all-to-all(bf16[8,2,13824]{2,1,0:T(2,128)(2,1)} %reshape.249), channel_id=1, replica_groups=mesh['frame'=8,'tok'=4] {'frame'}, dimensions={0} | all-to-all | bytes 884736 | tf_op jit(solution)/shard_map/all_to_all | solution.py:116
  322.5 3.8 reshape.250
  326.3 4.5 %copy.91 = bf16[1,768,288]{1,2,0:T(8,128)(2,1)} copy(bf16[1,768,288]{2,0,1:T(2,128)(2,1)} %bitcast.122) | data formatting | bytes 884736 | tf_op jit(solution)/shard_map/all_to_all | solution.py:116
  330.8 2.5 all_to_all.80
  334.0 6.5 %gather_fusion.1 = bf16[768]{0:T(1024)(128)(2,1)S(1)} fusion(bf16[8,256]{1,0:T(8,128)(2,1)S(1)} %fusion.28, s32[768]{0:T(1024)S(1)} %reshape.231), kind=kCustom, calls=%fused_computation.1 | custom fusion | bytes 9216 | tf_op jit(solution)/shard_map/jit(take_along_axis)/gather | solution.py:118
  340.5 28.3 %all-gather.2.cloned.1.call-done = bf16[8,96,1152]{1,0,2:T(8,128)(2,1)} async-done(((bf16[8,96,288]{1,0,2:T(8,128)(2,1)}), bf16[8,96,1152]{1,0,2:T(8,128)(2,1)}) %all-gather.2.cloned.1.call-update) | async-done | bytes 1769488 | tf_op jit(solution)/shard_map/all_gather | solution.py:117
  368.8 4.2 %copy.92 = bf16[8,96,1152]{2,1,0:T(8,128)(2,1)} copy(bf16[8,96,1152]{1,0,2:T(8,128)(2,1)} %all-gather.2.cloned.1.call-done) | data formatting | bytes 3538944 | tf_op jit(solution)/shard_map/all_gather | solution.py:117
  373.0 3.3 fusion.24
  (119 shorter events, 57.8 us)
Async XLA Ops:
  6.5 227.7 %copy-start = (bf16[1,1152,1152]{2,1,0:T(8,128)(2,1)S(1)}, bf16[1,1152,1152]{2,1,0:T(8,128)(2,1)}, u32[]{:S(2)}) copy-start(bf16[1,1152,1152]{2,1,0:T(8,128)(2,1)} %param.28) | copy-start | bytes 7962628
  8.8 13.9 %all-to-all-start = ((bf16[4,4,72,256]{3,2,1,0:T(8,128)(2,1)}), bf16[4,4,72,256]{3,2,1,0:T(8,128)(2,1)S(1)}, u32[]{:S(2)}, u32[]{:S(2)}) async-start(bf16[4,4,72,256]{3,2,1,0:T(8,128)(2,1)} %bitcast.128), calls=%async_computation | async-start | bytes 1179648 | tf_op jit(solution)/shard_map/all_to_all | solution.py:75
  14.0 15.2 %copy-start.5 = (s32[8,1,96]{2,1,0:T(1,128)S(1)}, s32[8,1,96]{2,1,0:T(1,128)}, u32[]{:S(2)}) copy-start(s32[8,1,96]{2,1,0:T(1,128)} %param.31) | copy-start | bytes 9220
  22.7 16.7 %copy-start.3 = (f32[1,4,1152]{2,1,0:T(4,128)S(1)}, f32[1,4,1152]{2,1,0:T(4,128)}, u32[]{:S(2)}) copy-start(f32[1,4,1152]{2,1,0:T(4,128)} %param.22) | copy-start | bytes 55300
  22.7 12.4 %all-to-all-start.1 = ((bf16[4,4,72,256]{3,2,1,0:T(8,128)(2,1)}), bf16[4,4,72,256]{3,2,1,0:T(8,128)(2,1)}, u32[]{:S(2)}, u32[]{:S(2)}) async-start(bf16[4,4,72,256]{3,2,1,0:T(8,128)(2,1)} %bitcast.127), calls=%async_computation.1 | async-start | bytes 1179648 | tf_op jit(solution)/shard_map/all_to_all | solution.py:76
  35.1 11.7 %all-to-all-start.2 = ((bf16[4,4,72,256]{3,2,1,0:T(8,128)(2,1)}), bf16[4,4,72,256]{3,2,1,0:T(8,128)(2,1)}, u32[]{:S(2)}, u32[]{:S(2)}) async-start(bf16[4,4,72,256]{3,2,1,0:T(8,128)(2,1)} %bitcast.126), calls=%async_computation.2 | async-start | bytes 1179648 | tf_op jit(solution)/shard_map/all_to_all | solution.py:77
  95.6 6.8 %copy-start.6 = (s32[8,1]{0,1:T(1,128)S(1)}, s32[8,1]{0,1:T(1,128)}, u32[]{:S(2)}) copy-start(s32[8,1]{0,1:T(1,128)} %param.30) | copy-start | bytes 100
  97.9 17.4 %copy-start.7 = (f32[1152]{0:T(1024)S(1)}, f32[1152]{0:T(1024)}, u32[]{:S(2)}) copy-start(f32[1152]{0:T(1024)} %param.24) | copy-start | bytes 13828
  97.9 15.9 %all-to-all-start.3 = ((bf16[1,4,72,1024]{2,1,0,3:T(4,128)(2,1)}), bf16[1,4,72,1024]{2,1,0,3:T(4,128)(2,1)}, u32[]{:S(2)}, u32[]{:S(2)}) async-start(bf16[1,4,72,1024]{2,1,0,3:T(4,128)(2,1)} %bitcast.123), calls=%async_computation.3 | async-start | bytes 2097152 | tf_op jit(solution)/shard_map/all_to_all | solution.py:80
  102.3 131.9 %all-reduce.2.cloned.1.call-start = ((), (), s32[]{:S(2)}) async-start(), calls=%async_computation.7 | async-start | bytes 3538944 | tf_op jit(solution)/shard_map/psum | solution.py:99
  118.4 1.0 copy-start.1
  172.0 0.7 copy-start.4
  172.1 116.0 %reduce-scatter.4.cloned.1.call-start = ((), (), s32[]{:S(2)}) async-start(), calls=%async_computation.9 | async-start | bytes 2211840
  255.4 113.4 %all-gather.2.cloned.1.call-start = ((), (), s32[]{:S(2)}) async-start(), calls=%async_computation.8 | async-start | bytes 2949120 | tf_op jit(solution)/shard_map/all_gather | solution.py:117
  326.3 7.4 %copy-start.2 = (bf16[1152,8]{0,1:T(8,128)(2,1)S(1)}, bf16[1152,8]{0,1:T(8,128)(2,1)}, u32[]{:S(2)}) copy-start(bf16[1152,8]{0,1:T(8,128)(2,1)} %param.25) | copy-start | bytes 55300
Sparse Core Ops, SparseCore 0:
  172.2 61.9 all-reduce.1
  255.5 32.4 reduce-scatter.3
  333.4 35.2 all-gather.1
where the time goes:
time: 385 us; the launch traced here: 383 us
  waiting for transfers between devices  147 us (38%)
  local copies, waits for them, and re-layouts  84.9 us (22%)
  blocking collectives  65.1 us (17%)
  matrix products  25.9 us (7%)
  starting transfers between devices  18.3 us (5%)
  loops' own time  14.9 us (4%)
  other arithmetic  13.9 us (4%)
  between operations  13.3 us (3%)
    psum x1, waiting for transfers between devices, per_device(): lax.psum(moved.astype(jnp.float32).astype(jnp.bfloat16), 'tok')  61.5 us
    all_to_all x1, blocking collectives, per_device(): lax.all_to_all(chosen, 'frame', split_axis=0, concat_axis=1, tiled=True)  46.8 us
    unnamed x4, waiting for transfers between devices  31.9 us
    unnamed x25, local copies, waits for them, and re-layouts  28.5 us
    all_gather x1, waiting for transfers between devices, per_device(): returned_rows = lax.all_gather(returned_cols, 'tok', axis=2, tiled=True)  28.3 us
    all_to_all x1, blocking collectives, per_device(): lax.all_to_all(expert_out, 'frame', split_axis=1, concat_axis=0, tiled=True)  18.3 us
    another operation x4, loops' own time, head_attention(): blocks = lax.map(one_block, starts)  14.8 us
    all_to_all x1, waiting for transfers between devices, per_device(): lax.all_to_all(attended, 'tok', split_axis=3, concat_axis=0, tiled=True)  11.4 us
  transfers between devices with their start and end apart: 7, of which 7 were waited for; matrix products, arithmetic and copies ran while one was open for 5% of the time, Pallas kernels for 0%

commit v1 on v0

--- a/solution.py
+++ b/solution.py
@@ -114,7 +114,7 @@
     )
     expert_out = (summed + bias_part[:, None, :]).astype(jnp.bfloat16)
     returned_cols = lax.all_to_all(expert_out, "frame", split_axis=1, concat_axis=0, tiled=True)
-    returned_rows = lax.all_gather(returned_cols, "tok", axis=2, tiled=True)
+    returned_rows = jnp.concatenate(lax.all_gather(returned_cols, "tok"), axis=2)
     mix_weight = jnp.take_along_axis(gate_values.T, safe_pos, axis=1)
     mix_weight = jnp.where(on_shard, mix_weight, jnp.zeros_like(mix_weight)).astype(jnp.bfloat16)
     targets = jnp.arange(tok_local, dtype=jnp.int32)

time: 385 us -> 385 us (level)
    all_to_all x2 -> x0, local copies, waits for them, and re-layouts: 6.99 us -> none  [per_device(): lax.all_to_all(expert_out, 'frame', split_axis=1, concat_axis=0, tiled=True)]
    another operation x0 -> x1, local copies, waits for them, and re-layouts: none -> 4.69 us  [per_device(): returned_rows.reshape(-1, model_width)]
    reshape x0 -> x1, local copies, waits for them, and re-layouts: none -> 4.53 us  [per_device(): jnp.concatenate(lax.all_gather(returned_cols, 'tok'), axis=2)]
    all_gather x1 -> x0, local copies, waits for them, and re-layouts: 4.22 us -> none  [per_device(): returned_rows = lax.all_gather(returned_cols, 'tok', axis=2, tiled=True)]
    unnamed x25 -> x26, local copies, waits for them, and re-layouts: 28.5 us -> 30.7 us
where the time goes in v1:
time: 385 us; the launch traced here: 383 us
  waiting for transfers between devices  147 us (38%)
  local copies, waits for them, and re-layouts  85 us (22%)
  blocking collectives  65.1 us (17%)
  matrix products  26 us (7%)
  starting transfers between devices  18.3 us (5%)
  loops' own time  14.9 us (4%)
  other arithmetic  13.9 us (4%)
  between operations  13.3 us (3%)
    psum x1, waiting for transfers between devices, per_device(): lax.psum(moved.astype(jnp.float32).astype(jnp.bfloat16), 'tok')  61.5 us
    all_to_all x1, blocking collectives, per_device(): lax.all_to_all(chosen, 'frame', split_axis=0, concat_axis=1, tiled=True)  46.8 us
    unnamed x4, waiting for transfers between devices  31.9 us
    unnamed x26, local copies, waits for them, and re-layouts  30.7 us
    all_gather x1, waiting for transfers between devices, per_device(): lax.all_gather(returned_cols, 'tok')  28.3 us
    all_to_all x1, blocking collectives, per_device(): lax.all_to_all(expert_out, 'frame', split_axis=1, concat_axis=0, tiled=True)  18.3 us
    another operation x4, loops' own time, head_attention(): blocks = lax.map(one_block, starts)  14.8 us
    all_to_all x1, waiting for transfers between devices, per_device(): lax.all_to_all(attended, 'tok', split_axis=3, concat_axis=0, tiled=True)  11.4 us
  transfers between devices with their start and end apart: 7, of which 7 were waited for; matrix products, arithmetic and copies ran while one was open for 5% of the time, Pallas kernels for 0%

profile of v1, /device:TPU:0, one launch (start us, length us, event | category | flops | bytes accessed | tf_op | source)
XLA Modules:
  0.0 383.1 jit_solution(17712531784272706513)
XLA Ops:
  8.8 5.2 %all-to-all-start = ((bf16[4,4,72,256]{3,2,1,0:T(8,128)(2,1)}), bf16[4,4,72,256]{3,2,1,0:T(8,128)(2,1)S(1)}, u32[]{:S(2)}, u32[]{:S(2)}) async-start(bf16[4,4,72,256]{3,2,1,0:T(8,128)(2,1)} %bitcast.133), calls=%async_computation | async-start | bytes 1179648 | tf_op jit(solution)/shard_map/all_to_all | solution.py:75
  16.1 6.6 %all-to-all-done = bf16[4,4,72,256]{3,2,1,0:T(8,128)(2,1)S(1)} async-done(((bf16[4,4,72,256]{3,2,1,0:T(8,128)(2,1)}), bf16[4,4,72,256]{3,2,1,0:T(8,128)(2,1)S(1)}, u32[]{:S(2)}, u32[]{:S(2)}) %all-to-all-start) | async-done | bytes 589856 | tf_op jit(solution)/shard_map/all_to_all | solution.py:75
  22.7 4.3 %all-to-all-start.1 = ((bf16[4,4,72,256]{3,2,1,0:T(8,128)(2,1)}), bf16[4,4,72,256]{3,2,1,0:T(8,128)(2,1)}, u32[]{:S(2)}, u32[]{:S(2)}) async-start(bf16[4,4,72,256]{3,2,1,0:T(8,128)(2,1)} %bitcast.132), calls=%async_computation.1 | async-start | bytes 1179648 | tf_op jit(solution)/shard_map/all_to_all | solution.py:76
  29.2 5.9 %all-to-all-done.1 = bf16[4,4,72,256]{3,2,1,0:T(8,128)(2,1)} async-done(((bf16[4,4,72,256]{3,2,1,0:T(8,128)(2,1)}), bf16[4,4,72,256]{3,2,1,0:T(8,128)(2,1)}, u32[]{:S(2)}, u32[]{:S(2)}) %all-to-all-start.1) | async-done | bytes 589856 | tf_op jit(solution)/shard_map/all_to_all | solution.py:76
  35.1 4.2 %all-to-all-start.2 = ((bf16[4,4,72,256]{3,2,1,0:T(8,128)(2,1)}), bf16[4,4,72,256]{3,2,1,0:T(8,128)(2,1)}, u32[]{:S(2)}, u32[]{:S(2)}) async-start(bf16[4,4,72,256]{3,2,1,0:T(8,128)(2,1)} %bitcast.131), calls=%async_computation.2 | async-start | bytes 1179648 | tf_op jit(solution)/shard_map/all_to_all | solution.py:77
  40.8 2.4 squeeze.27
  49.6 45.9 %while.21 = (s32[]{:T(128)}, bf16[4,72,1024]{2,1,0:T(8,128)(2,1)}, bf16[4,72,1024]{2,1,0:T(8,128)(2,1)}, bf16[4,72,1024]{2,1,0:T(8,128)(2,1)}, bf16[4,72,1024]{2...) while((s32[]{:T(128)}, bf16[4,72,1024]{2,1,0:T(8,128)(2,1)}, ...), condition=%wide.region_5.6_spmd, body=%wide.region_0.5_spmd.sunk | while | flops 155749376 | bytes 8513900 | solution.py:45
  51.6 8.6 %while.22 = (s32[]{:T(128)}, bf16[2,72,512]{2,1,0:T(8,128)(2,1)S(1)}, s32[2]{0:T(128)S(1)}, bf16[72,1024]{1,0:T(8,128)(2,1)S(1)}, bf16[72,1024]{1,0:T(8,128)(2,1...) while((s32[]{:T(128)}, bf16[2,72,512]{2,1,0:T(8,128)(2,1)S(1)}, ...), condition=%wide.region_4.4_spmd, body=%wide.region_1.3_spmd.sunk | while | flops 155749376 | bytes 6744219 | solution.py:40
  63.1 8.6 %while.22 = (s32[]{:T(128)}, bf16[2,72,512]{2,1,0:T(8,128)(2,1)S(1)}, s32[2]{0:T(128)S(1)}, bf16[72,1024]{1,0:T(8,128)(2,1)S(1)}, bf16[72,1024]{1,0:T(8,128)(2,1...) while((s32[]{:T(128)}, bf16[2,72,512]{2,1,0:T(8,128)(2,1)S(1)}, ...), condition=%wide.region_4.4_spmd, body=%wide.region_1.3_spmd.sunk | while | flops 155749376 | bytes 6744219 | solution.py:40
  74.6 8.6 %while.22 = (s32[]{:T(128)}, bf16[2,72,512]{2,1,0:T(8,128)(2,1)S(1)}, s32[2]{0:T(128)S(1)}, bf16[72,1024]{1,0:T(8,128)(2,1)S(1)}, bf16[72,1024]{1,0:T(8,128)(2,1...) while((s32[]{:T(128)}, bf16[2,72,512]{2,1,0:T(8,128)(2,1)S(1)}, ...), condition=%wide.region_4.4_spmd, body=%wide.region_1.3_spmd.sunk | while | flops 155749376 | bytes 6744219 | solution.py:40
  86.0 8.6 %while.22 = (s32[]{:T(128)}, bf16[2,72,512]{2,1,0:T(8,128)(2,1)S(1)}, s32[2]{0:T(128)S(1)}, bf16[72,1024]{1,0:T(8,128)(2,1)S(1)}, bf16[72,1024]{1,0:T(8,128)(2,1...) while((s32[]{:T(128)}, bf16[2,72,512]{2,1,0:T(8,128)(2,1)S(1)}, ...), condition=%wide.region_4.4_spmd, body=%wide.region_1.3_spmd.sunk | while | flops 155749376 | bytes 6744219 | solution.py:40
  95.6 2.3 copy.88
  97.9 4.4 %all-to-all-start.3 = ((bf16[1,4,72,1024]{2,1,0,3:T(4,128)(2,1)}), bf16[1,4,72,1024]{2,1,0,3:T(4,128)(2,1)}, u32[]{:S(2)}, u32[]{:S(2)}) async-start(bf16[1,4,72,1024]{2,1,0,3:T(4,128)(2,1)} %bitcast.126), calls=%async_computation.3 | async-start | bytes 2097152 | tf_op jit(solution)/shard_map/all_to_all | solution.py:80
  102.5 11.4 %all-to-all-done.3 = bf16[1,4,72,1024]{2,1,0,3:T(4,128)(2,1)} async-done(((bf16[1,4,72,1024]{2,1,0,3:T(4,128)(2,1)}), bf16[1,4,72,1024]{2,1,0,3:T(4,128)(2,1)}, u32[]{:S(2)}, u32[]{:S(2)}) %all-to-all-start.3) | async-done | bytes 589856 | tf_op jit(solution)/shard_map/all_to_all | solution.py:80
  115.4 3.0 fusion.44
  119.7 3.7 gather_fusion
  125.3 46.8 %all_to_all.87 = bf16[8,96,1152]{2,1,0:T(8,128)(2,1)} all-to-all(bf16[8,96,1152]{2,1,0:T(8,128)(2,1)S(1)} %select_select_fusion), channel_id=1, replica_groups=mesh['frame'=8,'tok'=4] {'frame'}, dimensions={0} | all-to-all | bytes 3538944 | tf_op jit(solution)/shard_map/all_to_all | solution.py:98
  172.8 61.5 %all-reduce.2.cloned.1.call-done = bf16[768,1152]{1,0:T(8,128)(2,1)} async-done(((bf16[768,1152]{1,0:T(8,128)(2,1)}), bf16[768,1152]{1,0:T(8,128)(2,1)}) %all-reduce.2.cloned.1.call-update) | async-done | bytes 1769488 | tf_op jit(solution)/shard_map/psum | solution.py:99
  234.2 8.8 %fusion.15 = bf16[1,768,1152]{2,1,0:T(8,128)(2,1)} fusion(bf16[1,1152,1152]{2,1,0:T(8,128)(2,1)S(1)} %copy-done, bf16[768,1152]{1,0:T(8,128)(2,1)} %all-reduce.2.cloned.1.call-done, bf16[1,1152,1152]{2,1,0:T(8,128)(2,1)} %param.26, f32[1152]{0:T(1024)S(1)} %reduce.5), kind=kOutput, calls=%fused_computation.29 | convolution fusion | flops 4086595584 | bytes 8851968 | tf_op jit(solution)/shard_map/erf,efd->erd/dot_general | solution.py:105
  243.0 8.8 %copy.101 = bf16[1,768,1152]{1,0,2:T(2,128)(2,1)} copy(bf16[1,768,1152]{2,1,0:T(8,128)(2,1)} %fusion.15) | data formatting | bytes 3538944
  251.9 3.5 copy.110
  256.2 31.8 %reduce-scatter.4.cloned.1.call-done = bf16[288,768]{1,0:T(8,128)(2,1)} async-done(((bf16[1152,768]{1,0:T(8,128)(2,1)}), bf16[288,768]{1,0:T(8,128)(2,1)}) %reduce-scatter.4.cloned.1.call-update) | async-done | bytes 442384
  290.4 4.6 %copy.94 = bf16[1,768,288]{2,0,1:T(2,128)(2,1)} copy(bf16[1,768,288]{1,2,0:T(8,128)(2,1)} %add_convert_fusion.1) | data formatting | bytes 884736 | tf_op jit(solution)/shard_map/convert_element_type | solution.py:115
  295.5 6.1 %reduce.13 = bf16[768,288]{1,0:T(8,128)(2,1)} reduce(bf16[768,1,288]{2,1,0:T(2,128)(2,1)} %bitcast.124, bf16[]{:T(256)} %broadcast.265), dimensions={1}, to_apply=%bitcast.95.reduce_sub_computation | reduce | bytes 884738
  301.6 2.6 reshape.250
  304.3 18.3 %all_to_all.88 = bf16[8,2,13824]{2,1,0:T(2,128)(2,1)} all-to-all(bf16[8,2,13824]{2,1,0:T(2,128)(2,1)} %reshape.250), channel_id=1, replica_groups=mesh['frame'=8,'tok'=4] {'frame'}, dimensions={0} | all-to-all | bytes 884736 | tf_op jit(solution)/shard_map/all_to_all | solution.py:116
  322.5 3.8 reshape.251
  329.2 6.5 %gather_fusion.1 = bf16[768]{0:T(1024)(128)(2,1)S(1)} fusion(bf16[8,256]{1,0:T(8,128)(2,1)S(1)} %fusion.28, s32[768]{0:T(1024)S(1)} %reshape.231), kind=kCustom, calls=%fused_computation.1 | custom fusion | bytes 9216 | tf_op jit(solution)/shard_map/jit(take_along_axis)/gather | solution.py:118
  335.7 28.3 %all-gather.2.cloned.1.call-done = bf16[4,8,96,288]{3,2,1,0:T(8,128)(2,1)} async-done(((bf16[1,8,96,288]{3,2,1,0:T(8,128)(2,1)}), bf16[4,8,96,288]{3,2,1,0:T(8,128)(2,1)}) %all-gather.2.cloned.1.call-update) | async-done | bytes 1769488 | tf_op jit(solution)/shard_map/all_gather | solution.py:117
  364.0 4.5 %copy.97 = bf16[8,96,4,288]{1,0,3,2:T(8,128)(2,1)} copy(bf16[8,96,4,288]{3,1,0,2:T(8,128)(2,1)} %bitcast.129) | data formatting | bytes 3538944 | tf_op jit(solution)/shard_map/reshape | solution.py:117
  368.5 4.7 %reshape_reshape.3 = bf16[768,1152]{0,1:T(8,128)(2,1)} reshape(bf16[8,96,4,288]{1,0,3,2:T(8,128)(2,1)} %copy.97) | data formatting | bytes 3538944 | tf_op jit(solution)/shard_map/reshape;reshape | solution.py:124
  373.2 3.4 fusion.24
  (119 shorter events, 57.6 us)
Async XLA Ops:
  6.5 227.7 %copy-start = (bf16[1,1152,1152]{2,1,0:T(8,128)(2,1)S(1)}, bf16[1,1152,1152]{2,1,0:T(8,128)(2,1)}, u32[]{:S(2)}) copy-start(bf16[1,1152,1152]{2,1,0:T(8,128)(2,1)} %param.28) | copy-start | bytes 7962628
  8.8 13.9 %all-to-all-start = ((bf16[4,4,72,256]{3,2,1,0:T(8,128)(2,1)}), bf16[4,4,72,256]{3,2,1,0:T(8,128)(2,1)S(1)}, u32[]{:S(2)}, u32[]{:S(2)}) async-start(bf16[4,4,72,256]{3,2,1,0:T(8,128)(2,1)} %bitcast.133), calls=%async_computation | async-start | bytes 1179648 | tf_op jit(solution)/shard_map/all_to_all | solution.py:75
  14.0 15.2 %copy-start.5 = (s32[8,1,96]{2,1,0:T(1,128)S(1)}, s32[8,1,96]{2,1,0:T(1,128)}, u32[]{:S(2)}) copy-start(s32[8,1,96]{2,1,0:T(1,128)} %param.31) | copy-start | bytes 9220
  22.7 16.7 %copy-start.3 = (f32[1,4,1152]{2,1,0:T(4,128)S(1)}, f32[1,4,1152]{2,1,0:T(4,128)}, u32[]{:S(2)}) copy-start(f32[1,4,1152]{2,1,0:T(4,128)} %param.22) | copy-start | bytes 55300
  22.7 12.4 %all-to-all-start.1 = ((bf16[4,4,72,256]{3,2,1,0:T(8,128)(2,1)}), bf16[4,4,72,256]{3,2,1,0:T(8,128)(2,1)}, u32[]{:S(2)}, u32[]{:S(2)}) async-start(bf16[4,4,72,256]{3,2,1,0:T(8,128)(2,1)} %bitcast.132), calls=%async_computation.1 | async-start | bytes 1179648 | tf_op jit(solution)/shard_map/all_to_all | solution.py:76
  35.1 11.7 %all-to-all-start.2 = ((bf16[4,4,72,256]{3,2,1,0:T(8,128)(2,1)}), bf16[4,4,72,256]{3,2,1,0:T(8,128)(2,1)}, u32[]{:S(2)}, u32[]{:S(2)}) async-start(bf16[4,4,72,256]{3,2,1,0:T(8,128)(2,1)} %bitcast.131), calls=%async_computation.2 | async-start | bytes 1179648 | tf_op jit(solution)/shard_map/all_to_all | solution.py:77
  95.6 6.8 %copy-start.6 = (s32[8,1]{0,1:T(1,128)S(1)}, s32[8,1]{0,1:T(1,128)}, u32[]{:S(2)}) copy-start(s32[8,1]{0,1:T(1,128)} %param.30) | copy-start | bytes 100
  97.9 17.4 %copy-start.7 = (f32[1152]{0:T(1024)S(1)}, f32[1152]{0:T(1024)}, u32[]{:S(2)}) copy-start(f32[1152]{0:T(1024)} %param.24) | copy-start | bytes 13828
  97.9 15.9 %all-to-all-start.3 = ((bf16[1,4,72,1024]{2,1,0,3:T(4,128)(2,1)}), bf16[1,4,72,1024]{2,1,0,3:T(4,128)(2,1)}, u32[]{:S(2)}, u32[]{:S(2)}) async-start(bf16[1,4,72,1024]{2,1,0,3:T(4,128)(2,1)} %bitcast.126), calls=%async_computation.3 | async-start | bytes 2097152 | tf_op jit(solution)/shard_map/all_to_all | solution.py:80
  102.3 131.9 %all-reduce.2.cloned.1.call-start = ((), (), s32[]{:S(2)}) async-start(), calls=%async_computation.7 | async-start | bytes 3538944 | tf_op jit(solution)/shard_map/psum | solution.py:99
  118.4 1.0 copy-start.1
  172.0 0.7 copy-start.4
  172.1 116.0 %reduce-scatter.4.cloned.1.call-start = ((), (), s32[]{:S(2)}) async-start(), calls=%async_computation.9 | async-start | bytes 2211840
  255.4 108.6 %all-gather.2.cloned.1.call-start = ((), (), s32[]{:S(2)}) async-start(), calls=%async_computation.8 | async-start | bytes 2949120 | tf_op jit(solution)/shard_map/all_gather | solution.py:117
  322.5 6.4 %copy-start.2 = (bf16[1152,8]{0,1:T(8,128)(2,1)S(1)}, bf16[1152,8]{0,1:T(8,128)(2,1)}, u32[]{:S(2)}) copy-start(bf16[1152,8]{0,1:T(8,128)(2,1)} %param.25) | copy-start | bytes 55300
Sparse Core Ops, SparseCore 0:
  172.2 61.9 all-reduce.1
  255.5 32.4 reduce-scatter.3
  328.6 35.2 all-gather.1
